TPU v7x, 32 devices: a whole 2x2x4 slice. The times are simulated.
32 devices in a mesh: rep: 4 (over y, x), shard: 8 (over z, core).
Axes of the slice: x: 2, y: 2, z: 4, core: 2. Of those that a mesh axis runs over, the one named last changes fastest.
Arguments:
- tokens: bfloat16 [8192, 1024], P(('rep', 'shard')), may hold values from -6 to 6
- cotangent: bfloat16 [8192, 1024], P(('rep', 'shard')), may hold values from -6 to 6
- positions: int32 [8192], P(('rep', 'shard')), may hold values from 0 to 255, as said below
- counts: int32 [32], P(('rep', 'shard')), may hold values from 128 to 256, as said below
- attn_weight: bfloat16 [1024, 3072], P('shard'), may hold values from -0.75 to 0.75
- ffn_weight: bfloat16 [4608, 3, 1024], P('shard'), may hold values from -0.1875 to 0.1875
- gains: bfloat16 [2, 1024], P(None, 'shard'), may hold values from 0.099609375 to 1.8984375
- qk_gains: bfloat16 [2, 64], P(None, 'shard'), as said below
Outputs:
- output: bfloat16 [8192, 1024], P(('rep', 'shard'))
- grad_input: bfloat16 [8192, 1024], P(('rep', 'shard'))
- grad_attn: float32 [1024, 3072], P('shard')
- grad_ffn: float32 [4608, 3, 1024], P('shard')
- grad_gains: float32 [2, 1024], P(None, 'shard')
- grad_qk: float32 [2, 64], P(None, 'shard')
Inputs may be any that keep to these rules, and one draw needn't show every extreme that they name: `counts`: one device holds 256 real tokens and another 128 in every draw. `positions`: sequences lie whole inside one device's block of 256 slots, one after another; slots at or past the block's count hold 0. `qk_gains`: positive scales.
All inputs are finite; a program needn't handle non-finite values.
Results may differ from a plain program's by a relative error of at most 0.018.
Values may be sent and summed in bfloat16 or wider, within the bound.
A program may use at most 320 MiB of HBM per device.

v0:
```python
import jax
import jax.numpy as jnp
from jax import lax
from jax.sharding import PartitionSpec as P

QUERY_HEADS = 16
KEY_VALUE_HEADS = 8
HEAD_WIDTH = 64
QUERY_FEATURES = 1024
KEY_FEATURES = 512
EPS = 1e-05
THETA = 1000000.0


def rope_tables(positions, head_size):
    half = head_size // 2
    freq = THETA ** (-2.0 * jnp.arange(half, dtype=jnp.float32) / head_size)
    angle = positions.astype(jnp.float32)[:, None] * freq[None, :]
    return (jnp.cos(angle), jnp.sin(angle))


def apply_rotation(vectors, cosine_table, sine_table, sign):
    half = vectors.shape[-1] // 2
    upper = vectors[..., :half]
    lower = vectors[..., half:]
    cos_b = cosine_table[:, None, :]
    sin_b = sine_table[:, None, :] * sign
    return jnp.concatenate([upper * cos_b - lower * sin_b, lower * cos_b + upper * sin_b], axis=-1)


def rms_back(grad_normed, unit, inverse, gain):
    inner = grad_normed * gain
    return inverse * (inner - unit * jnp.mean(inner * unit, axis=-1, keepdims=True))


def times_trans(left, right):
    return lax.dot_general(
        left, right, (((1,), (1,)), ((), ())), preferred_element_type=jnp.float32
    )


def trans_times(left, right):
    return lax.dot_general(
        left, right, (((0,), (0,)), ((), ())), preferred_element_type=jnp.float32
    )


def local(tokens, cotangent, positions, counts, attn_weight, ffn_weight, gains, qk_gains):
    token_rows = tokens.shape[0]
    width = QUERY_FEATURES + 2 * KEY_FEATURES
    replica_group = QUERY_HEADS // KEY_VALUE_HEADS
    scale = HEAD_WIDTH ** (-0.5)
    full_attn, full_gains, full_qk = (
        lax.all_gather(attn_weight, "shard", axis=0, tiled=True),
        lax.all_gather(gains, "shard", axis=1, tiled=True),
        lax.all_gather(qk_gains, "shard", axis=1, tiled=True),
    )
    index = jnp.arange(token_rows, dtype=jnp.int32)
    valid = (index < counts[0]).astype(jnp.float32)[:, None]
    allowed = (index[None, :] <= index[:, None]) & (index[None, :] >= (index - positions)[:, None])
    gain_one = full_gains[0].astype(jnp.float32)
    gain_two = full_gains[1].astype(jnp.float32)
    query_gain = full_qk[0].astype(jnp.float32)
    k_gain = full_qk[1].astype(jnp.float32)
    wide = tokens.astype(jnp.float32)
    inv_one = lax.rsqrt(jnp.mean(wide * wide, axis=-1, keepdims=True) + EPS)
    unit_one = wide * inv_one
    normed_one = (unit_one * gain_one).astype(jnp.bfloat16)
    projected_output = jnp.dot(normed_one, full_attn[:, :width], preferred_element_type=jnp.float32)
    query = projected_output[:, :QUERY_FEATURES].reshape(token_rows, QUERY_HEADS, HEAD_WIDTH)
    key_rows = projected_output[:, QUERY_FEATURES : QUERY_FEATURES + KEY_FEATURES].reshape(
        token_rows, KEY_VALUE_HEADS, HEAD_WIDTH
    )
    value_rows = (
        projected_output[:, QUERY_FEATURES + KEY_FEATURES :]
        .reshape(token_rows, KEY_VALUE_HEADS, HEAD_WIDTH)
        .astype(jnp.bfloat16)
    )
    q_inv = lax.rsqrt(jnp.mean(query * query, axis=-1, keepdims=True) + EPS)
    query_unit = query * q_inv
    k_inv = lax.rsqrt(jnp.mean(key_rows * key_rows, axis=-1, keepdims=True) + EPS)
    k_unit = key_rows * k_inv
    cosine_table, sine_table = rope_tables(positions, HEAD_WIDTH)
    query_rotated = (
        apply_rotation(query_unit * query_gain, cosine_table, sine_table, 1.0)
        .astype(jnp.bfloat16)
        .reshape(token_rows, KEY_VALUE_HEADS, replica_group, HEAD_WIDTH)
    )
    key_r = apply_rotation(k_unit * k_gain, cosine_table, sine_table, 1.0).astype(jnp.bfloat16)
    scores = (
        jnp.einsum("qhgd,khd->hgqk", query_rotated, key_r, preferred_element_type=jnp.float32)
        * scale
    )
    masked = jnp.where(allowed, scores, -1e30)
    top = jnp.max(masked, axis=-1, keepdims=True)
    lse = top + jnp.log(jnp.sum(jnp.exp(masked - top), axis=-1, keepdims=True))
    probs = jnp.exp(masked - lse).astype(jnp.bfloat16)
    attended = jnp.einsum(
        "hgqk,khd->qhgd", probs, value_rows, preferred_element_type=jnp.float32
    ).astype(jnp.bfloat16)
    attended_flat = attended.reshape(token_rows, QUERY_FEATURES)
    mid = wide + times_trans(attended_flat, full_attn[:, width:])
    inv_two = lax.rsqrt(jnp.mean(mid * mid, axis=-1, keepdims=True) + EPS)
    unit_two = mid * inv_two
    normed_two = (unit_two * gain_two).astype(jnp.bfloat16)
    piece = lax.all_gather(ffn_weight, "shard", axis=0, tiled=True)
    gate = times_trans(normed_two, piece[:, 0, :])
    up_proj = times_trans(normed_two, piece[:, 1, :])
    hidden_piece = (gate * jax.nn.sigmoid(gate) * up_proj).astype(jnp.bfloat16)
    total = jnp.dot(hidden_piece, piece[:, 2, :], preferred_element_type=jnp.float32)
    gate_all = gate
    up_all = up_proj
    result = ((mid + total) * valid).astype(jnp.bfloat16)
    cot = (cotangent.astype(jnp.float32) * valid).astype(jnp.bfloat16)
    piece = lax.all_gather(ffn_weight, "shard", axis=0, tiled=True)
    gate = gate_all
    up_proj = up_all
    sig = jax.nn.sigmoid(gate)
    d_hidden = times_trans(cot, piece[:, 2, :])
    d_gate = (d_hidden * up_proj * sig * (1.0 + gate * (1.0 - sig))).astype(jnp.bfloat16)
    d_up = (d_hidden * gate * sig).astype(jnp.bfloat16)
    d_normed = jnp.dot(d_gate, piece[:, 0, :], preferred_element_type=jnp.float32) + jnp.dot(
        d_up, piece[:, 1, :], preferred_element_type=jnp.float32
    )
    grad_ffn = lax.psum_scatter(
        jnp.stack(
            [
                trans_times(d_gate, normed_two),
                trans_times(d_up, normed_two),
                trans_times(hidden_piece, cot),
            ],
            axis=1,
        ).astype(jnp.bfloat16),
        "shard",
        scatter_dimension=0,
        tiled=True,
    ).astype(jnp.float32)
    grad_two = jnp.sum(d_normed * unit_two, axis=0)
    d_mid = cot.astype(jnp.float32) + rms_back(d_normed, unit_two, inv_two, gain_two)
    d_mid_b = d_mid.astype(jnp.bfloat16)
    back_attn = lax.all_gather(attn_weight, "shard", axis=0, tiled=True)
    attended_gradient = jnp.dot(
        d_mid_b, back_attn[:, width:], preferred_element_type=jnp.float32
    ).astype(jnp.bfloat16)
    attention_gradient = attended_gradient.reshape(
        token_rows, KEY_VALUE_HEADS, replica_group, HEAD_WIDTH
    )
    scores_again = (
        jnp.einsum("qhgd,khd->hgqk", query_rotated, key_r, preferred_element_type=jnp.float32)
        * scale
    )
    probs_wide = jnp.exp(jnp.where(allowed, scores_again, -1e30) - lse)
    d_probs = jnp.einsum(
        "qhgd,khd->hgqk", attention_gradient, value_rows, preferred_element_type=jnp.float32
    )
    delta = jnp.sum(attention_gradient.astype(jnp.float32) * attended.astype(jnp.float32), axis=-1)
    delta = jnp.transpose(delta, (1, 2, 0))[..., None]
    d_scores = (probs_wide * (d_probs - delta) * scale).astype(jnp.bfloat16)
    d_query_r = jnp.einsum(
        "hgqk,khd->qhgd", d_scores, key_r, preferred_element_type=jnp.float32
    ).reshape(token_rows, QUERY_HEADS, HEAD_WIDTH)
    d_key_r = jnp.einsum(
        "hgqk,qhgd->khd", d_scores, query_rotated, preferred_element_type=jnp.float32
    )
    d_value = jnp.einsum(
        "hgqk,qhgd->khd", probs, attention_gradient, preferred_element_type=jnp.float32
    )
    d_q_scaled = apply_rotation(d_query_r, cosine_table, sine_table, -1.0)
    d_k_scaled = apply_rotation(d_key_r, cosine_table, sine_table, -1.0)
    grad_q = jnp.sum(d_q_scaled * query_unit, axis=(0, 1))
    grad_k = jnp.sum(d_k_scaled * k_unit, axis=(0, 1))
    d_query = rms_back(d_q_scaled, query_unit, q_inv, query_gain)
    d_key = rms_back(d_k_scaled, k_unit, k_inv, k_gain)
    d_projected = jnp.concatenate(
        [
            d_query.reshape(token_rows, QUERY_FEATURES),
            d_key.reshape(token_rows, KEY_FEATURES),
            d_value.reshape(token_rows, KEY_FEATURES),
        ],
        axis=1,
    ).astype(jnp.bfloat16)
    d_normed_one = times_trans(d_projected, back_attn[:, :width])
    grad_one = jnp.sum(d_normed_one * unit_one, axis=0)
    grad_input = (d_mid + rms_back(d_normed_one, unit_one, inv_one, gain_one)).astype(jnp.bfloat16)
    grad_attn = lax.psum_scatter(
        jnp.concatenate(
            [trans_times(normed_one, d_projected), trans_times(d_mid_b, attended_flat)], axis=1
        ).astype(jnp.bfloat16),
        "shard",
        scatter_dimension=0,
        tiled=True,
    ).astype(jnp.float32)
    grad_gains, grad_qk = (
        lax.psum_scatter(jnp.stack([grad_one, grad_two]), "shard", scatter_dimension=1, tiled=True),
        lax.psum_scatter(jnp.stack([grad_q, grad_k]), "shard", scatter_dimension=1, tiled=True),
    )
    grad_attn, grad_ffn, grad_gains, grad_qk = (
        lax.psum(grad_attn.astype(jnp.bfloat16), "rep").astype(jnp.float32),
        lax.psum(grad_ffn.astype(jnp.bfloat16), "rep").astype(jnp.float32),
        lax.psum(grad_gains.astype(jnp.bfloat16), "rep").astype(jnp.float32),
        lax.psum(grad_qk.astype(jnp.bfloat16), "rep").astype(jnp.float32),
    )
    return (result, grad_input, grad_attn, grad_ffn, grad_gains, grad_qk)


def solution(mesh):
    in_specs = (
        P(("rep", "shard"), None),
        P(("rep", "shard"), None),
        P(("rep", "shard")),
        P(("rep", "shard")),
        P("shard", None),
        P("shard", None, None),
        P(None, "shard"),
        P(None, "shard"),
    )
    out_specs = (
        P(("rep", "shard"), None),
        P(("rep", "shard"), None),
        P("shard", None),
        P("shard", None, None),
        P(None, "shard"),
        P(None, "shard"),
    )
    return jax.shard_map(local, mesh=mesh, in_specs=in_specs, out_specs=out_specs, check_vma=False)
```

profile of v0, /device:TPU:0, one launch (start us, length us, event | category | flops | bytes accessed | tf_op | source)
XLA Modules:
  0.0 899.5 jit_solution(8453053964591804986)
XLA Ops:
  8.7 13.5 %all-gather = bf16[8,8,2]{1,2,0:T(2,128)(2,1)S(1)} all-gather(bf16[1,8,2]{1,2,0:T(2,128)(2,1)S(1)} %bitcast.186), channel_id=1, replica_groups=mesh['rep'=4,'shard'=8] {'shard'}, dimensions={0}, use_global_device_ids=true | all-gather | bytes 288 | tf_op jit(solution)/shard_map/all_gather | solution.py:56
  23.1 9.1 %all_gather.14 = bf16[2,1024]{1,0:T(2,128)(2,1)S(1)} all-gather(bf16[2,128]{1,0:T(2,128)(2,1)S(1)} %copy-done.45), channel_id=1, replica_groups=mesh['rep'=4,'shard'=8] {'shard'}, dimensions={1}, use_global_device_ids=true | all-gather | bytes 4608 | tf_op jit(solution)/shard_map/all_gather | solution.py:55
  33.9 43.2 %all-gather.4.cloned.1.call-done = bf16[1024,3072]{1,0:T(8,128)(2,1)} async-done(((bf16[128,3072]{1,0:T(8,128)(2,1)}), bf16[1024,3072]{1,0:T(8,128)(2,1)}) %all-gather.4.cloned.1.call-update) | async-done | bytes 6291472 | tf_op jit(solution)/shard_map/all_gather | solution.py:54
  77.1 3.5 fusion.15
  90.6 3.1 multiply_reduce_fusion.5
  94.8 228.2 %all-gather.6.cloned.1.call-done = bf16[4608,3,1024]{2,0,1:T(8,128)(2,1)} async-done(((bf16[576,3,1024]{2,0,1:T(8,128)(2,1)}), bf16[4608,3,1024]{2,0,1:T(8,128)(2,1)}) %all-gather.6.cloned.1.call-update) | async-done | bytes 28311568 | tf_op jit(solution)/shard_map/all_gather | solution.py:106
  323.0 5.2 fusion.1
  328.3 8.6 fusion.3
  336.8 9.0 multiply_convert_fusion
  345.8 6.9 fusion
  352.8 6.2 multiply_reduce_fusion.1
  359.4 3.1 fusion.32
  365.9 4.3 fusion.35
  383.7 2.7 copy.84
  387.5 2.6 copy.86
  391.7 2.4 multiply_reduce_fusion
  396.3 3.3 pad_maximum_fusion.1
  400.6 6.9 fusion.7
  407.4 5.1 fusion.6
  412.6 5.2 fusion.8
  417.8 19.8 %pad_maximum_fusion = bf16[4608,3,1024]{2,0,1:T(8,128)(2,1)} fusion(bf16[4608,1,1024]{2,0,1:T(8,128)(2,1)} %fusion.8, bf16[4608,1,1024]{2,0,1:T(8,128)(2,1)} %fusion.7, bf16[4608,1,1024]{2,0,1:T(8,128)(2,1)} %fusion.6), kind=kLoop, calls=%fused_computation | loop fusion | flops 28311552 | bytes 56623104 | tf_op jit(solution)/shard_map/stack | solution.py:126
  438.8 4.6 fusion.42
  444.6 23.0 %reduce-scatter.7.cloned.1.call-done = bf16[128,3072]{1,0:T(8,128)(2,1)} async-done(((bf16[1024,3072]{1,0:T(8,128)(2,1)}), bf16[128,3072]{1,0:T(8,128)(2,1)}) %reduce-scatter.7.cloned.1.call-update) | async-done | bytes 786448 | tf_op jit(solution)/shard_map/reduce_scatter | solution.py:185
  467.6 277.4 %reduce-scatter.9.cloned.1.call-done = bf16[576,3,1024]{2,0,1:T(8,128)(2,1)} async-done(((bf16[4608,3,1024]{2,0,1:T(8,128)(2,1)}), bf16[576,3,1024]{2,0,1:T(8,128)(2,1)}) %reduce-scatter.9.cloned.1.call-update) | async-done | bytes 3538960 | tf_op jit(solution)/shard_map/reduce_scatter | solution.py:125
  746.5 13.7 %all-reduce = bf16[2,64]{1,0:T(2,128)(2,1)S(1)} all-reduce(f32[2,64]{1,0:T(2,128)S(1)} %pad_maximum_fusion.11), channel_id=5, replica_groups=mesh['rep'=4,'shard'=8] {'shard'}, use_global_device_ids=true, to_apply=%region_23.24.clone | all-reduce | flops 128 | bytes 768
  760.3 2.3 fusion.41
  762.6 7.9 fusion.31
  770.5 6.6 reduce-scatter.11.cloned.1.call-done
  778.0 9.9 %all-reduce.1 = (bf16[2,128]{1,0:T(2,128)(2,1)S(1)}, bf16[2,8]{1,0:T(2,128)(2,1)S(1)}) all-reduce(bf16[2,128]{1,0:T(2,128)(2,1)S(1)} %copy.108, bf16[2,8]{1,0:T(2,128)(2,1)S(1)} %dynamic-slice_convert_fusion), channel_id=1, replica_groups=mesh['rep'=4,'shard'=8] {'rep'}, use_global_device_ids=true, to_apply=%region_18.19 | all-reduce | flops 272 | bytes 1088 | tf_op jit(solution)/shard_map/psum | solution.py:200
  789.0 95.4 %all-reduce.5.cloned.1.call-done = (bf16[128,3072]{1,0:T(8,128)(2,1)}, bf16[576,3,1024]{2,0,1:T(8,128)(2,1)}) async-done(((bf16[128,3072]{1,0:T(8,128)(2,1)}, bf16[576,3,1024]{2,0,1:T(8,128)(2,1)}), (bf16[128,3072]{1,0:T(8,128)(2,1)}, bf16[576,3,1024]{2,0,1:T(8,128)(2,1)})) %all-reduce.5.cloned.1.call-update) | async-done | bytes 4325392 | tf_op jit(solution)/shard_map/psum | solution.py:198
  884.4 2.4 convert_element_type.149
  886.8 5.8 convert_element_type.150
  (179 shorter events, 42.7 us)
Async XLA Ops:
  7.2 16.0 %copy-start.45 = (bf16[2,128]{1,0:T(2,128)(2,1)S(1)}, bf16[2,128]{1,0:T(2,128)(2,1)}, u32[]{:S(2)}) copy-start(bf16[2,128]{1,0:T(2,128)(2,1)} %param.14) | copy-start | bytes 1540
  7.2 25.6 %copy-start.15 = (bf16[256,1024]{1,0:T(8,128)(2,1)S(1)}, bf16[256,1024]{1,0:T(8,128)(2,1)}, u32[]{:S(2)}) copy-start(bf16[256,1024]{1,0:T(8,128)(2,1)} %param.8) | copy-start | bytes 1572868
  7.2 25.8 %copy-start.43 = (s32[256]{0:T(256)S(1)}, s32[256]{0:T(256)}, u32[]{:S(2)}) copy-start(s32[256]{0:T(256)} %param.10) | copy-start | bytes 3076
  7.2 69.9 %all-gather.4.cloned.1.call-start = ((), (), s32[]{:S(2)}) async-start(), calls=%async_computation.3 | async-start | bytes 7077888 | tf_op jit(solution)/shard_map/all_gather | solution.py:54
  7.9 315.1 %all-gather.6.cloned.1.call-start = ((), (), s32[]{:S(2)}) async-start(), calls=%async_computation.4 | async-start | bytes 31850496 | tf_op jit(solution)/shard_map/all_gather | solution.py:106
  8.7 458.9 %reduce-scatter.7.cloned.1.call-start = ((), (), s32[]{:S(2)}) async-start(), calls=%async_computation.5 | async-start | bytes 7077888 | tf_op jit(solution)/shard_map/reduce_scatter | solution.py:185
  33.0 47.6 %copy-start.38 = (f32[256]{0:T(256)}, f32[256]{0:T(256)S(1)}, u32[]{:S(2)}) copy-start(f32[256]{0:T(256)S(1)} %add_rsqrt_fusion.3) | copy-start | bytes 3076
  94.8 233.4 %copy-start.3 = (bf16[256,1024]{1,0:T(8,128)(2,1)}, bf16[256,1024]{1,0:T(8,128)(2,1)S(1)}, u32[]{:S(2)}) copy-start(bf16[256,1024]{1,0:T(8,128)(2,1)S(1)} %multiply_convert_fusion.5) | copy-start | bytes 1572868
  328.2 8.6 copy-start.19
  328.3 8.6 copy-start.41
  345.8 6.9 copy-start.10
  345.8 6.9 copy-start.12
  345.8 6.9 copy-start.6
  359.0 7.0 copy-start.37
  364.5 5.7 copy-start.9
  364.5 5.7 copy-start.14
  364.5 5.7 copy-start.30
  364.6 5.7 copy-start.34
  383.7 6.3 copy-start.2
  387.5 7.4 copy-start.39
  390.1 4.8 copy-start.17
  390.1 4.8 copy-start.31
  399.5 345.5 %reduce-scatter.9.cloned.1.call-start = ((), (), s32[]{:S(2)}) async-start(), calls=%async_computation.6 | async-start | bytes 31850496 | tf_op jit(solution)/shard_map/reduce_scatter | solution.py:125
  400.6 6.9 copy-start.11
  407.4 5.2 copy-start.13
  407.4 5.2 copy-start.20
  407.4 5.2 copy-start.42
  437.6 5.8 copy-start.40
  437.6 339.5 %reduce-scatter.11.cloned.1.call-start = ((), (), s32[]{:S(2)}) async-start(), calls=%async_computation.7 | async-start | bytes 589824
  443.4 301.6 %copy-start.46 = (u32[32]{0:T(128)S(1)}, u32[32]{0:T(128)}, u32[]{:S(2)}) copy-start(u32[32]{0:T(128)} %constant.39) | copy-start | bytes 388
  443.4 319.2 %copy-start.7 = (f32[256,1024]{1,0:T(8,128)S(1)}, f32[256,1024]{1,0:T(8,128)}, u32[]{:S(2)}) copy-start(f32[256,1024]{1,0:T(8,128)} %copy-done.5) | copy-start | bytes 3145732
  444.5 439.9 %all-reduce.5.cloned.1.call-start = ((), (), s32[]{:S(2)}) async-start(), calls=%async_computation.8 | async-start | bytes 8650752 | tf_op jit(solution)/shard_map/psum | solution.py:198
  (21 other events, 40.0 us)
Sparse Core Ops, SparseCore 0:
  9.7 67.3 all-gather.3
  78.7 244.2 all-gather.5
  399.7 67.8 reduce-scatter.6
  469.8 275.1 reduce-scatter.8
  747.1 29.9 reduce-scatter.10
  780.5 103.8 all-reduce.4
where the time goes:
time: 900 us; the launch traced here: 899 us
  waiting for transfers between devices  675 us (75%)
  matrix products  90.3 us (10%)
  other arithmetic  47.9 us (5%)
  blocking collectives  46.2 us (5%)
  local copies, waits for them, and re-layouts  23.5 us (3%)
  between operations  16.1 us (2%)
    reduce_scatter x1, waiting for transfers between devices, local(): lax.psum_scatter(jnp.stack([trans_times(d_gate, normed_two), trans_times(...  277 us
    all_gather x1, waiting for transfers between devices, local(): piece = lax.all_gather(ffn_weight, 'shard', axis=0, tiled=True)  228 us
    psum x1, waiting for transfers between devices, local(): lax.psum(grad_attn.astype(jnp.bfloat16), 'rep').astype(jnp.float32)  95.4 us
    all_gather x1, waiting for transfers between devices, local(): lax.all_gather(attn_weight, 'shard', axis=0, tiled=True)  43.2 us
    dot_general x5, matrix products, times_trans(): lax.dot_general(left, right, (((1,), (1,)), ((), ())), preferred_element_...  30.4 us
    reduce_scatter x1, waiting for transfers between devices, local(): lax.psum_scatter(jnp.concatenate([trans_times(normed_one, d_projected), t...  23 us
    dot_general x5, matrix products, trans_times(): lax.dot_general(left, right, (((0,), (0,)), ((), ())), preferred_element_...  20.6 us
    another operation x1, other arithmetic, local(): jnp.stack([trans_times(d_gate, normed_two), trans_times(d_up, normed_two)...  19.8 us
  transfers between devices with their start and end apart: 6, of which 6 were waited for; matrix products, arithmetic and copies ran while one was open for 8% of the time, Pallas kernels for 0%

commit v1 on v0

--- a/solution.py
+++ b/solution.py
@@ -195,7 +195,7 @@
         lax.psum_scatter(jnp.stack([grad_q, grad_k]), "shard", scatter_dimension=1, tiled=True),
     )
     grad_attn, grad_ffn, grad_gains, grad_qk = (
-        lax.psum(grad_attn.astype(jnp.bfloat16), "rep").astype(jnp.float32),
+        jnp.sum(lax.all_gather(grad_attn.astype(jnp.bfloat16), "rep"), axis=0).astype(jnp.float32),
         lax.psum(grad_ffn.astype(jnp.bfloat16), "rep").astype(jnp.float32),
         lax.psum(grad_gains.astype(jnp.bfloat16), "rep").astype(jnp.float32),
         lax.psum(grad_qk.astype(jnp.bfloat16), "rep").astype(jnp.float32),

time: 900 us -> 931 us (1.034)
  waiting for transfers between devices: 675 us -> 704 us
    all_gather x0 -> x1, waiting for transfers between devices: none -> 31.7 us  [local(): lax.all_gather(grad_attn.astype(jnp.bfloat16), 'rep')]
  transfers between devices with their start and end apart: 6 -> 7, of which waited for: 6 -> 7; matrix products, arithmetic and copies ran while one was open for 8% -> 8% of each run, Pallas kernels for 0% -> 0%
where the time goes in v1:
time: 931 us; the launch traced here: 930 us
  waiting for transfers between devices  704 us (76%)
  matrix products  90.4 us (10%)
  other arithmetic  49.3 us (5%)
  blocking collectives  46.3 us (5%)
  local copies, waits for them, and re-layouts  23.5 us (3%)
  between operations  16.1 us (2%)
    reduce_scatter x1, waiting for transfers between devices, local(): lax.psum_scatter(jnp.stack([trans_times(d_gate, normed_two), trans_times(...  277 us
    all_gather x1, waiting for transfers between devices, local(): piece = lax.all_gather(ffn_weight, 'shard', axis=0, tiled=True)  228 us
    psum x1, waiting for transfers between devices, local(): lax.psum(grad_ffn.astype(jnp.bfloat16), 'rep').astype(jnp.float32)  92.9 us
    all_gather x1, waiting for transfers between devices, local(): lax.all_gather(attn_weight, 'shard', axis=0, tiled=True)  43.2 us
    all_gather x1, waiting for transfers between devices, local(): lax.all_gather(grad_attn.astype(jnp.bfloat16), 'rep')  31.7 us
    dot_general x5, matrix products, times_trans(): lax.dot_general(left, right, (((1,), (1,)), ((), ())), preferred_element_...  30.5 us
    reduce_scatter x1, waiting for transfers between devices, local(): lax.psum_scatter(jnp.concatenate([trans_times(normed_one, d_projected), t...  23 us
    dot_general x5, matrix products, trans_times(): lax.dot_general(left, right, (((0,), (0,)), ((), ())), preferred_element_...  20.6 us
  transfers between devices with their start and end apart: 7, of which 7 were waited for; matrix products, arithmetic and copies ran while one was open for 8% of the time, Pallas kernels for 0%

profile of v1, /device:TPU:0, one launch (start us, length us, event | category | flops | bytes accessed | tf_op | source)
XLA Modules:
  0.0 930.3 jit_solution(18243505765342746141)
XLA Ops:
  8.7 13.5 %all-gather.1 = bf16[8,8,2]{1,2,0:T(2,128)(2,1)S(1)} all-gather(bf16[1,8,2]{1,2,0:T(2,128)(2,1)S(1)} %bitcast.188), channel_id=1, replica_groups=mesh['rep'=4,'shard'=8] {'shard'}, dimensions={0}, use_global_device_ids=true | all-gather | bytes 288 | tf_op jit(solution)/shard_map/all_gather | solution.py:56
  23.1 9.1 all_gather.20
  33.9 43.2 %all-gather.6.cloned.1.call-done = bf16[1024,3072]{1,0:T(8,128)(2,1)} async-done(((bf16[128,3072]{1,0:T(8,128)(2,1)}), bf16[1024,3072]{1,0:T(8,128)(2,1)}) %all-gather.6.cloned.1.call-update) | async-done | bytes 6291472 | tf_op jit(solution)/shard_map/all_gather | solution.py:54
  77.1 3.5 fusion.15
  90.6 3.1 multiply_reduce_fusion.5
  94.8 228.2 %all-gather.8.cloned.1.call-done = bf16[4608,3,1024]{2,0,1:T(8,128)(2,1)} async-done(((bf16[576,3,1024]{2,0,1:T(8,128)(2,1)}), bf16[4608,3,1024]{2,0,1:T(8,128)(2,1)}) %all-gather.8.cloned.1.call-update) | async-done | bytes 28311568 | tf_op jit(solution)/shard_map/all_gather | solution.py:106
  323.0 5.2 fusion.1
  328.3 8.6 fusion.3
  336.8 9.0 multiply_convert_fusion
  345.8 6.9 fusion
  352.8 6.2 multiply_reduce_fusion.1
  359.4 3.1 fusion.32
  366.0 4.4 fusion.35
  383.7 2.7 copy.84
  387.5 2.6 copy.86
  391.7 2.4 multiply_reduce_fusion
  396.3 3.3 pad_maximum_fusion.1
  400.6 6.9 fusion.7
  407.5 5.1 fusion.6
  412.6 5.2 fusion.8
  417.8 19.8 %pad_maximum_fusion = bf16[4608,3,1024]{2,0,1:T(8,128)(2,1)} fusion(bf16[4608,1,1024]{2,0,1:T(8,128)(2,1)} %fusion.8, bf16[4608,1,1024]{2,0,1:T(8,128)(2,1)} %fusion.7, bf16[4608,1,1024]{2,0,1:T(8,128)(2,1)} %fusion.6), kind=kLoop, calls=%fused_computation | loop fusion | flops 28311552 | bytes 56623104 | tf_op jit(solution)/shard_map/stack | solution.py:126
  438.9 4.6 fusion.42
  444.7 23.0 %reduce-scatter.7.cloned.1.call-done = bf16[128,3072]{1,0:T(8,128)(2,1)} async-done(((bf16[1024,3072]{1,0:T(8,128)(2,1)}), bf16[128,3072]{1,0:T(8,128)(2,1)}) %reduce-scatter.7.cloned.1.call-update) | async-done | bytes 786448 | tf_op jit(solution)/shard_map/reduce_scatter | solution.py:185
  467.7 277.3 %reduce-scatter.9.cloned.1.call-done = bf16[576,3,1024]{2,0,1:T(8,128)(2,1)} async-done(((bf16[4608,3,1024]{2,0,1:T(8,128)(2,1)}), bf16[576,3,1024]{2,0,1:T(8,128)(2,1)}) %reduce-scatter.9.cloned.1.call-update) | async-done | bytes 3538960 | tf_op jit(solution)/shard_map/reduce_scatter | solution.py:125
  746.5 13.7 %all-reduce = bf16[2,64]{1,0:T(2,128)(2,1)S(1)} all-reduce(f32[2,64]{1,0:T(2,128)S(1)} %pad_maximum_fusion.11), channel_id=6, replica_groups=mesh['rep'=4,'shard'=8] {'shard'}, use_global_device_ids=true, to_apply=%region_23.24.clone | all-reduce | flops 128 | bytes 768
  762.6 7.9 fusion.31
  770.5 6.6 reduce-scatter.11.cloned.1.call-done
  778.0 10.0 %all-reduce.1 = (bf16[2,128]{1,0:T(2,128)(2,1)S(1)}, bf16[2,8]{1,0:T(2,128)(2,1)S(1)}) all-reduce(bf16[2,128]{1,0:T(2,128)(2,1)S(1)} %copy.108, bf16[2,8]{1,0:T(2,128)(2,1)S(1)} %dynamic-slice_convert_fusion), channel_id=1, replica_groups=mesh['rep'=4,'shard'=8] {'rep'}, use_global_device_ids=true, to_apply=%region_18.19 | all-reduce | flops 272 | bytes 1088 | tf_op jit(solution)/shard_map/psum | solution.py:200
  789.1 31.7 %all-gather.10.cloned.1.call-done = bf16[512,3072]{1,0:T(8,128)(2,1)} async-done(((bf16[128,3072]{1,0:T(8,128)(2,1)}), bf16[512,3072]{1,0:T(8,128)(2,1)}) %all-gather.10.cloned.1.call-update) | async-done | bytes 3145744 | tf_op jit(solution)/shard_map/all_gather | solution.py:198
  820.9 2.5 reduce_sum.162
  824.7 92.9 %all-reduce.4.cloned.1.call-done = bf16[576,3,1024]{2,0,1:T(8,128)(2,1)} async-done(((bf16[576,3,1024]{2,0,1:T(8,128)(2,1)}), bf16[576,3,1024]{2,0,1:T(8,128)(2,1)}) %all-reduce.4.cloned.1.call-update) | async-done | bytes 3538960 | tf_op jit(solution)/shard_map/psum | solution.py:199
  917.6 5.8 convert_element_type.152
  (183 shorter events, 46.3 us)
Async XLA Ops:
  7.2 16.0 %copy-start.45 = (bf16[2,128]{1,0:T(2,128)(2,1)S(1)}, bf16[2,128]{1,0:T(2,128)(2,1)}, u32[]{:S(2)}) copy-start(bf16[2,128]{1,0:T(2,128)(2,1)} %param.14) | copy-start | bytes 1540
  7.2 25.6 %copy-start.15 = (bf16[256,1024]{1,0:T(8,128)(2,1)S(1)}, bf16[256,1024]{1,0:T(8,128)(2,1)}, u32[]{:S(2)}) copy-start(bf16[256,1024]{1,0:T(8,128)(2,1)} %param.8) | copy-start | bytes 1572868
  7.2 25.8 %copy-start.43 = (s32[256]{0:T(256)S(1)}, s32[256]{0:T(256)}, u32[]{:S(2)}) copy-start(s32[256]{0:T(256)} %param.10) | copy-start | bytes 3076
  7.2 69.9 %all-gather.6.cloned.1.call-start = ((), (), s32[]{:S(2)}) async-start(), calls=%async_computation.3 | async-start | bytes 7077888 | tf_op jit(solution)/shard_map/all_gather | solution.py:54
  7.9 315.1 %all-gather.8.cloned.1.call-start = ((), (), s32[]{:S(2)}) async-start(), calls=%async_computation.4 | async-start | bytes 31850496 | tf_op jit(solution)/shard_map/all_gather | solution.py:106
  8.7 458.9 %reduce-scatter.7.cloned.1.call-start = ((), (), s32[]{:S(2)}) async-start(), calls=%async_computation.5 | async-start | bytes 7077888 | tf_op jit(solution)/shard_map/reduce_scatter | solution.py:185
  33.0 47.6 %copy-start.38 = (f32[256]{0:T(256)}, f32[256]{0:T(256)S(1)}, u32[]{:S(2)}) copy-start(f32[256]{0:T(256)S(1)} %add_rsqrt_fusion.3) | copy-start | bytes 3076
  94.8 233.4 %copy-start.3 = (bf16[256,1024]{1,0:T(8,128)(2,1)}, bf16[256,1024]{1,0:T(8,128)(2,1)S(1)}, u32[]{:S(2)}) copy-start(bf16[256,1024]{1,0:T(8,128)(2,1)S(1)} %multiply_convert_fusion.5) | copy-start | bytes 1572868
  328.2 8.6 copy-start.19
  328.3 8.6 copy-start.41
  345.8 6.9 copy-start.10
  345.8 6.9 copy-start.12
  345.8 6.9 copy-start.6
  359.0 7.0 copy-start.37
  364.6 5.8 copy-start.9
  364.6 5.8 copy-start.14
  364.6 5.8 copy-start.30
  364.6 5.8 copy-start.34
  383.7 6.3 copy-start.2
  387.5 7.4 copy-start.39
  390.1 4.8 copy-start.31
  399.6 345.5 %reduce-scatter.9.cloned.1.call-start = ((), (), s32[]{:S(2)}) async-start(), calls=%async_computation.6 | async-start | bytes 31850496 | tf_op jit(solution)/shard_map/reduce_scatter | solution.py:125
  400.6 6.9 copy-start.11
  407.4 5.1 copy-start.13
  407.4 5.1 copy-start.20
  407.4 5.1 copy-start.42
  437.6 5.9 copy-start.40
  437.7 339.5 %reduce-scatter.11.cloned.1.call-start = ((), (), s32[]{:S(2)}) async-start(), calls=%async_computation.9 | async-start | bytes 589824
  443.5 301.5 %copy-start.46 = (u32[32]{0:T(128)S(1)}, u32[32]{0:T(128)}, u32[]{:S(2)}) copy-start(u32[32]{0:T(128)} %constant.41) | copy-start | bytes 388
  443.5 319.1 %copy-start.7 = (f32[256,1024]{1,0:T(8,128)S(1)}, f32[256,1024]{1,0:T(8,128)}, u32[]{:S(2)}) copy-start(f32[256,1024]{1,0:T(8,128)} %copy-done.5) | copy-start | bytes 3145732
  444.6 376.2 %all-gather.10.cloned.1.call-start = ((), (), s32[]{:S(2)}) async-start(), calls=%async_computation.8 | async-start | bytes 3932160 | tf_op jit(solution)/shard_map/all_gather | solution.py:198
  467.6 449.9 %all-reduce.4.cloned.1.call-start = ((), (), s32[]{:S(2)}) async-start(), calls=%async_computation.7 | async-start | bytes 7077888 | tf_op jit(solution)/shard_map/psum | solution.py:199
  (22 other events, 44.8 us)
Sparse Core Ops, SparseCore 0:
  9.7 67.3 all-gather.5
  78.7 244.2 all-gather.7
  399.7 67.8 reduce-scatter.6
  469.8 275.1 reduce-scatter.8
  747.1 29.9 reduce-scatter.10
  778.8 41.9 all-gather.9
  824.0 93.4 all-reduce.3
